TPU v7x, 256 devices: a whole 4x4x8 slice. The times are simulated.
256 devices in a mesh: gx: 8 (over z_hi, core), gy: 32 (over y, z_lo, x).
Axes of the slice: x: 4, y: 4, z: 8 (z_hi: 4, z_lo: 2; z = z_hi * 2 + z_lo), core: 2. Of those that a mesh axis runs over, the one named last changes fastest.
Arguments:
- density: float32 [256, 16, 4096], P('gx', None, 'gy'), may hold values from 0.5 to 2
- velocity: float32 [3, 256, 16, 4096], P(None, 'gx', None, 'gy'), may hold values from -1.2 to 1.2
- bfield: float32 [3, 256, 16, 4096], P(None, 'gx', None, 'gy'), may hold values from -1.2 to 1.2
- pressure: float32 [256, 16, 4096], P('gx', None, 'gy'), may hold values from 0.5 to 2
- shear_shift: int32 [], replicated, may hold values from 0 to 4095
- remap_weight: int32 [], replicated, may hold values from 0 to 65535
Outputs:
- state: float32 [8, 256, 16, 4096], P(None, 'gx', None, 'gy')
All inputs are finite; a program needn't handle non-finite values.
Results may differ from a plain program's by a relative error of at most 0.0003.
Values sent between devices are 32-bit elements; how exact they have to be, the bound alone decides.
A program may use at most 128 MiB of HBM per device.

v0:
```python
import functools

import jax
import jax.numpy as jnp
from jax import lax
from jax.experimental import pallas as pl
from jax.experimental.pallas import tpu as pltpu
from jax.sharding import PartitionSpec as P

GAMMA = 5.0 / 3.0
SHEAR_Q = 1.5
TIME_STEP = 0.03
WEIGHT_SCALE = 1.0 / 65536.0
TINY = 1e-30
MESH = pl.DeviceIdType.MESH
DIGITS = {32: ((4, 1), (2, 4), (4, 8)), 8: ((2, 1), (2, 2), (2, 4))}
CUTS = (2, 12, 19, 28)


def limited(upper, lower):
    return jnp.minimum(jnp.maximum(upper, jnp.minimum(lower, 0.0)), jnp.maximum(lower, 0.0))


def side_flux(state, n):
    rho, v, b, p = state[0], state[1:4], state[4:7], state[7]
    a, c = [t for t in range(3) if t != n]
    m = [rho * v[t] for t in range(3)]
    vn, bn = v[n], b[n]
    bn2 = bn * bn
    bt2 = b[a] * b[a] + b[c] * b[c]
    b2 = bt2 + bn2
    hb2 = 0.5 * b2
    pg = p + 0.5 * (p + (m[0] * v[0] + m[1] * v[1] + m[2] * v[2]))
    energy = pg + hb2
    fba = vn * b[a] - bn * v[a]
    fbc = vn * b[c] - bn * v[c]
    flux = [None] * 8
    flux[0] = m[n]
    flux[1 + n] = m[n] * vn - bn2 + (p + hb2)
    flux[1 + a] = m[n] * v[a] - bn * b[a]
    flux[1 + c] = m[n] * v[c] - bn * b[c]
    flux[4 + a] = fba
    flux[4 + c] = fbc
    flux[7] = (pg + p) * vn + (b[a] * fba + b[c] * fbc)
    gp = GAMMA * p
    total = gp + b2
    spread = gp - b2
    inner = spread * spread + (4.0 * GAMMA * p) * bt2
    twice = total + inner * lax.rsqrt(jnp.maximum(inner, TINY))
    fast = twice * lax.rsqrt(jnp.maximum((rho + rho) * twice, TINY))
    return flux, [rho, *m, *b, energy], jnp.abs(vn) + fast


def face_flux(left, right, n):
    fl, ul, sl = side_flux(left, n)
    fr, ur, sr = side_flux(right, n)
    speed = jnp.maximum(sl, sr)
    out = []
    for k in range(8):
        jump = speed * (ur[k] - ul[k])
        out.append(-jump if fl[k] is None else (fl[k] + fr[k]) - jump)
    return out


def to_primitive(u):
    inv = 1.0 / u[0]
    v = [u[k] * inv for k in (1, 2, 3)]
    kin = u[1] * v[0] + u[2] * v[1] + u[3] * v[2]
    mag = u[4] * u[4] + u[5] * u[5] + u[6] * u[6]
    return [u[0], *v, u[4], u[5], u[6], (GAMMA - 1.0) * (u[7] - 0.5 * (kin + mag))]


def kernel(
    nx, ny, shift_ref, weight_ref, rho_ref, vel_ref, mag_ref, pre_ref, out_ref,
    u0, u1, w, wh, sd, sl, sf, pack, patch, xg, yg, st00, st01, st02, st10, st11, st12, ts, tb,
    xs, xr, ys, yr, cs, cr, tsem, trec,
):
    rows, nz, wide = rho_ref.shape
    half = nz // 2
    total_x = nx * rows
    total_y = ny * wide
    omega = 1.0 / (SHEAR_Q * total_x)
    digits = DIGITS[ny]
    stages = ((st00, st01, st02), (st10, st11, st12))
    gx = lax.axis_index("gx")
    gy = lax.axis_index("gy")
    first = gx == 0
    last = gx == nx - 1
    edge = jnp.logical_or(first, last)
    other = jnp.where(first, nx - 1, 0)
    north = lax.rem(gy + 1, ny)
    south = lax.rem(gy + ny - 1, ny)
    mine = [lax.rem(lax.div(gy, stride), radix) for radix, stride in digits]
    lane = lax.broadcasted_iota(jnp.int32, (2, half, wide), 2)
    quad = jnp.bitwise_and(lane, 3)
    group = lax.shift_right_logical(lane, 2)
    inside = jnp.logical_and(lane >= 2, lane < wide - 2)

    def digit_peer(stage, step):
        radix, stride = digits[stage]
        digit = lax.rem(mine[stage] + step, radix)
        return digit, gy + (digit - mine[stage]) * stride

    barrier = pltpu.get_barrier_semaphore()

    def greet(x, y):
        pl.semaphore_signal(barrier, inc=1, device_id=(x, y), device_id_type=MESH)

    greet(gx, north)
    greet(gx, south)

    @pl.when(gx > 0)
    def _():
        greet(gx - 1, gy)

    @pl.when(gx < nx - 1)
    def _():
        greet(gx + 1, gy)

    far = 3 + sum(radix - 1 for radix, _ in digits)

    @pl.when(edge)
    def _():
        for stage in range(3):
            for step in range(1, digits[stage][0]):
                greet(gx, digit_peer(stage, step)[1])
        for y in (south, gy, north):
            greet(other, y)

    def await_greetings():
        pl.semaphore_wait(barrier, jnp.where(edge, 3 + far, 4))

    def remote(src, dst, send, recv, x, y):
        return pltpu.make_async_remote_copy(
            src_ref=src, dst_ref=dst, send_sem=send, recv_sem=recv, device_id=(x, y), device_id_type=MESH
        )

    def radial(i):
        return (gx * rows + i).astype(jnp.float32) + (0.5 - 0.5 * total_x)

    def put_primitive(i, prim):
        for k in range(8):
            w[k, i + 2] = prim[k]
            wh[k, i + 2] = 0.5 * prim[k]

    def collect(i, prim, packs):
        turn = jnp.bitwise_and(4 * i + 4, wide - 1)
        here = group == i
        after = group == jnp.bitwise_and(i + 1, wide // 4 - 1)
        moved = [pltpu.roll(prim[k], turn, 2) for k in range(8)]
        left = [jnp.where(after, moved[k], packs[k]) for k in range(8)]
        right = [jnp.where(here, moved[k], packs[8 + k]) for k in range(8)]
        return (*left, *right)

    def store_packs(sec, packs):
        for k in range(8):
            pack[sec, 0, k] = pltpu.roll(packs[k], wide - 4, 2)
            pack[sec, 1, k] = packs[8 + k]

    def start_row(i, packs):
        def load(ref, *lead):
            return jnp.stack([ref[(*lead, i, pl.ds(z, half, stride=2), slice(None))] for z in range(2)])

        rho = load(rho_ref)
        v = [load(vel_ref, 0), load(vel_ref, 1) - SHEAR_Q * omega * radial(i), load(vel_ref, 2)]
        b = [load(mag_ref, k) for k in range(3)]
        p = load(pre_ref)
        m = [rho * v[k] for k in range(3)]
        kin = m[0] * v[0] + m[1] * v[1] + m[2] * v[2]
        mag = b[0] * b[0] + b[1] * b[1] + b[2] * b[2]
        energy = p * (1.0 / (GAMMA - 1.0)) + 0.5 * (kin + mag)
        for k, value in enumerate([rho, *m, *b, energy]):
            u0[k, i] = value
        prim = [rho, *v, *b, p]
        put_primitive(i, prim)
        return collect(i, prim, packs)

    def merged(i, ref, k):
        back = pltpu.roll(patch[k], jnp.bitwise_and(wide - 2 - 4 * i, wide - 1), 2)
        return ref[k, i] + jnp.where(inside, 0.0, back)

    def middle_row(i, packs):
        u = [merged(i, u1, k) for k in range(8)]
        for k in range(8):
            u1[k, i] = u[k]
        prim = to_primitive(u)
        put_primitive(i, prim)
        return collect(i, prim, packs)

    def final_row(i, carry):
        for k in range(8):
            value = merged(i, u0, k)
            for z in range(2):
                out_ref[k, i, pl.ds(z, half, stride=2), :] = value[z]
        return carry

    def z_up(x):
        return jnp.stack([x[1], pltpu.roll(x[0], half - 1, 0)])

    def z_down(x):
        return jnp.stack([pltpu.roll(x[1], 1, 0), x[0]])

    def y_up(x):
        return pltpu.roll(x, wide - 1, 2)

    def y_down(x):
        return pltpu.roll(x, 1, 2)

    def periodic(whole, halved, n, up, down):
        left, right = [], []
        for k in range(8):
            d = up(halved[k]) - halved[k]
            h = limited(d, down(d))
            left.append(whole[k] + h)
            right.append(up(whole[k] - h))
        face = face_flux(left, right, n)
        return [f - down(f) for f in face]

    def x_face(i):
        left, right = [], []
        for k in range(8):
            d = wh[k, i + 4] - wh[k, i + 3]
            h = limited(d, sd[k])
            here = w[k, i + 3]
            left.append(sl[k])
            right.append(here - h)
            sd[k] = d
            sl[k] = here + h
        return face_flux(left, right, 0)

    def x_begin(i):
        for k in range(8):
            before = wh[k, i + 1] - wh[k, i]
            d = wh[k, i + 2] - wh[k, i + 1]
            sd[k] = d
            sl[k] = w[k, i + 1] + limited(d, before)
        face = x_face(i - 1)
        for k in range(8):
            sf[k] = face[k]

    def main_row(sec, i, carry):
        whole = [w[k, i + 2] for k in range(8)]
        halved = [wh[k, i + 2] for k in range(8)]
        dz = periodic(whole, halved, 2, z_up, z_down)
        dy = periodic(whole, halved, 1, y_up, y_down)
        fx = x_face(i)
        change = []
        for k in range(8):
            change.append((dz[k] + jnp.where(inside, dy[k], 0.0)) + (fx[k] - sf[k]))
            sf[k] = fx[k]
        ref = u1 if sec else u0
        u = [ref[k, i] for k in range(8)]
        step = 0.5 * TIME_STEP if sec else TIME_STEP
        r = radial(i)
        pull = (2.0 * SHEAR_Q * omega * omega * step) * r
        source = {
            1: (2.0 * omega * step) * u[2] + pull * u[0],
            2: (-2.0 * omega * step) * u[1],
            7: pull * u[1],
        }
        for k in range(8):
            base = 0.5 * (u0[k, i] + u[k]) if sec else u[k]
            value = base - (0.5 * step) * change[k]
            if k in source:
                value = value + source[k]
            (u0 if sec else u1)[k, i] = value
        return carry

    def edge_patch(sec):
        step = 0.5 * TIME_STEP if sec else TIME_STEP

        def turned(x, by):
            return x if by % wide == 0 else pltpu.roll(x, by % wide, 2)

        def rates(low, high, base):
            left, right = [], []
            for k in range(8):
                col = []
                for t in range(-1, 3):
                    start = t - base
                    take = quad < -start
                    if start >= 0:
                        col.append(turned(high[k], -start))
                    elif start == -4:
                        col.append(low[k])
                    elif start < -4:
                        col.append(turned(low[k], -4 - start))
                    else:
                        col.append(jnp.where(take, turned(low[k], -4 - start), turned(high[k], -start)))
                d = [0.5 * (col[t + 1] - col[t]) for t in range(3)]
                left.append(col[1] + limited(d[1], d[0]))
                right.append(col[2] - limited(d[2], d[1]))
            face = face_flux(left, right, 1)
            return [f - pltpu.roll(f, 1, 2) for f in face]

        low_side = rates([yg[sec, 0, k] for k in range(8)], [pack[sec, 0, k] for k in range(8)], 2)
        high_side = rates([pack[sec, 1, k] for k in range(8)], [yg[sec, 1, k] for k in range(8)], 4)
        for k in range(8):
            both = jnp.where(quad < 2, pltpu.roll(high_side[k], wide - 2, 2), low_side[k])
            patch[k] = (-0.5 * step) * both

    shift = shift_ref[0]
    weight = weight_ref[0].astype(jnp.float32) * WEIGHT_SCALE
    out_shift = jnp.where(first, total_y - 1 - shift, shift)
    in_shift = jnp.where(first, shift, total_y - 1 - shift)
    in_weight = jnp.where(first, weight, 1.0 - weight)
    blocks = lax.div(out_shift, wide)
    picks = []
    for d, (radix, _) in enumerate(digits):
        part = lax.rem(blocks, radix)
        picks.append(lax.rem(mine[d] - part + radix, radix))
        blocks = lax.div(blocks, radix) + (mine[d] < part).astype(jnp.int32)

    def stage_copies(sec, stage, incoming):
        ref = stages[sec][stage]
        copies = []
        for step in range(1, digits[stage][0]):
            digit, y = digit_peer(stage, step)
            slot = digit if incoming else mine[stage]
            copies.append(
                remote(
                    ref.at[mine[stage]], ref.at[slot],
                    cs.at[sec, stage, step - 1], cr.at[sec, stage, slot], gx, y,
                )
            )
        return copies

    def transit_copies(sec):
        return [
            remote(ts.at[sec], tb.at[sec, 0], tsem.at[sec, 0], trec.at[sec, 0], other, gy),
            remote(ts.at[sec], tb.at[sec, 1], tsem.at[sec, 1], trec.at[sec, 1], other, north),
        ]

    def chain_start(sec, u):
        @pl.when(first)
        def _():
            for k in range(8):
                stages[sec][0][mine[0], k] = u[k, 0:2]

        @pl.when(last)
        def _():
            for k in range(8):
                stages[sec][0][mine[0], k] = u[k, rows - 2 : rows]

        @pl.when(edge)
        def _():
            for copy in stage_copies(sec, 0, False):
                copy.start()

    def chain_step(sec, stage):
        @pl.when(edge)
        def _():
            for copy in stage_copies(sec, stage, True):
                copy.wait_recv()
            for k in range(8):
                value = stages[sec][stage][picks[stage], k]
                if stage < 2:
                    stages[sec][stage + 1][mine[stage + 1], k] = value
                else:
                    ts[sec, k] = value
            for copy in stage_copies(sec, stage + 1, False) if stage < 2 else transit_copies(sec):
                copy.start()

    def chain_end(sec):
        @pl.when(edge)
        def _():
            for copy in transit_copies(sec):
                copy.wait_recv()
            inner = lax.rem(in_shift, wide)
            src = lax.broadcasted_iota(jnp.int32, (wide, wide), 0)
            dst = lax.broadcasted_iota(jnp.int32, (wide, wide), 1)
            gap = dst - src - inner
            near = jnp.where(gap == 0, 1.0 - in_weight, 0.0) + jnp.where(gap == 1, in_weight, 0.0)
            back = jnp.where(gap == -wide, 1.0 - in_weight, 0.0) + jnp.where(gap == 1 - wide, in_weight, 0.0)
            flat = (8 * 2 * 2 * half, wide)

            def times(x, m):
                return jnp.dot(x, m, precision=lax.Precision.HIGHEST, preferred_element_type=jnp.float32)

            ghost = times(tb[sec, 0].reshape(flat), near) + times(tb[sec, 1].reshape(flat), back)
            ghost = ghost.reshape(8, 2, 2, half, wide)
            delta = jnp.where(first, 1.0, -1.0)
            start = jnp.where(first, 0, rows + 2)
            for j in range(2):
                u = [ghost[k, j] for k in range(8)]
                momentum = u[2] + u[0] * delta
                u[7] = u[7] + u[2] * delta + 0.5 * u[0]
                u[2] = momentum
                put_primitive(start + j - 2, to_primitive(u))

    def x_copy(sec, side, incoming):
        away = gx - 1 if side == 0 else gx + 1
        own = w.at[:, 2:4] if side == 0 else w.at[:, rows : rows + 2]
        slot = side if incoming else 1 - side
        return remote(own, xg.at[sec, slot], xs.at[sec, side], xr.at[sec, slot], away, gy)

    def y_copy(sec, side, incoming):
        away = south if side == 0 else north
        slot = side if incoming else 1 - side
        return remote(pack.at[sec, side], yg.at[sec, slot], ys.at[sec, side], yr.at[sec, slot], gx, away)

    def on_side(side, do):
        pl.when(gx > 0 if side == 0 else gx < nx - 1)(do)

    def outer_row(t):
        return jnp.where(t < 2, t, t + rows - 4)

    empty = tuple(jnp.zeros((2, half, wide), jnp.float32) for _ in range(16))

    for sec in range(2):
        one_row = middle_row if sec else start_row
        packs = lax.fori_loop(0, 4, lambda t, c: one_row(outer_row(t), c), empty)
        if sec == 0:
            await_greetings()
        chain_start(sec, u1 if sec else u0)
        for side in range(2):
            on_side(side, lambda: x_copy(sec, side, False).start())
        packs = lax.fori_loop(2, rows - 2, one_row, packs)
        store_packs(sec, packs)
        x_begin(2)
        for side in range(2):
            y_copy(sec, side, False).start()
        row = functools.partial(main_row, sec)
        cuts = [min(c * rows // 32, rows - 2) for c in CUTS] + [rows - 2]
        cuts[0] = 2
        for stage in range(3):
            lax.fori_loop(cuts[stage], cuts[stage + 1], row, 0)
            chain_step(sec, stage)
        lax.fori_loop(cuts[3], cuts[4], row, 0)
        for side in range(2):
            y_copy(sec, side, True).wait_recv()
        edge_patch(sec)
        for side in range(2):

            def take():
                x_copy(sec, side, True).wait_recv()
                for k in range(8):
                    value = xg[sec, side, k]
                    start = 0 if side == 0 else rows + 2
                    w[k, start : start + 2] = value
                    wh[k, start : start + 2] = 0.5 * value

            on_side(side, take)
        chain_end(sec)
        lax.fori_loop(rows - 2, rows, row, 0)
        x_begin(0)
        lax.fori_loop(0, 2, row, 0)
        for side in range(2):
            on_side(side, lambda: x_copy(sec, side, False).wait_send())
            y_copy(sec, side, False).wait_send()
    lax.fori_loop(0, rows, final_row, 0)

    @pl.when(edge)
    def _():
        for sec in range(2):
            for stage in range(3):
                for copy in stage_copies(sec, stage, False):
                    copy.wait_send()
            for copy in transit_copies(sec):
                copy.wait_send()


def solution(mesh):
    nx, ny = mesh.shape["gx"], mesh.shape["gy"]

    def on_device(density, velocity, bfield, pressure, shear_shift, remap_weight):
        rows, nz, wide = density.shape
        half = nz // 2
        tile = (2, half, wide)
        radices = [radix for radix, _ in DIGITS[ny]]
        slab = (8, 2, *tile)
        f32 = jnp.float32
        dma = pltpu.SemaphoreType.DMA
        vmem = pl.BlockSpec(memory_space=pltpu.VMEM)
        smem = pl.BlockSpec(memory_space=pltpu.SMEM)
        return pl.pallas_call(
            functools.partial(kernel, nx, ny),
            out_shape=jax.ShapeDtypeStruct((8, rows, nz, wide), f32),
            in_specs=[smem, smem, vmem, vmem, vmem, vmem],
            out_specs=vmem,
            scratch_shapes=[
                pltpu.VMEM((8, rows, *tile), f32),
                pltpu.VMEM((8, rows, *tile), f32),
                pltpu.VMEM((8, rows + 4, *tile), f32),
                pltpu.VMEM((8, rows + 4, *tile), f32),
                pltpu.VMEM((8, *tile), f32),
                pltpu.VMEM((8, *tile), f32),
                pltpu.VMEM((8, *tile), f32),
                pltpu.VMEM((2, 2, 8, *tile), f32),
                pltpu.VMEM((8, *tile), f32),
                pltpu.VMEM((2, 2, *slab), f32),
                pltpu.VMEM((2, 2, 8, *tile), f32),
                *[pltpu.VMEM((radix, *slab), f32) for radix in radices * 2],
                pltpu.VMEM((2, *slab), f32),
                pltpu.VMEM((2, 2, *slab), f32),
                dma((2, 2)),
                dma((2, 2)),
                dma((2, 2)),
                dma((2, 2)),
                dma((2, 3, 3)),
                dma((2, 3, 4)),
                dma((2, 2)),
                dma((2, 2)),
            ],
            compiler_params=pltpu.CompilerParams(
                collective_id=0, has_side_effects=True, vmem_limit_bytes=60 * 1024 * 1024
            ),
        )(shear_shift.reshape(1), remap_weight.reshape(1), density, velocity, bfield, pressure)

    placed = (
        P("gx", None, "gy"),
        P(None, "gx", None, "gy"),
        P(None, "gx", None, "gy"),
        P("gx", None, "gy"),
        P(),
        P(),
    )
    return jax.shard_map(
        on_device, mesh=mesh, in_specs=placed, out_specs=P(None, "gx", None, "gy"), check_vma=False
    )
```

profile of v0, /device:TPU:8, one launch (start us, length us, event | category | flops | bytes accessed | tf_op | source)
XLA Modules:
  0.0 75.4 jit_solution(11229872037840006960)
XLA Ops:
  1.3 71.0 %shard_map.64 = f32[8,32,16,128]{3,2,1,0:T(8,128)} custom-call(s32[1]{0:T(128)} %bitcast.2.shift_ref, s32[1]{0:T(128)} %bitcast.3.weight_ref, f32[32,16,128]{2,1,0:T(8,128)} %rho_ref.1, f32[3,32,16,128]{3,2,1,0:T(8,128)} %vel_ref.1, f32[3,32,16,128]{3,2,1,0:T(8,128)} %mag_ref.1, f32[32,16,128]{2,1,0:T(8,128)} %pre_ref.1), custom_call_target="tpu_custom_call" | custom-call | tf_op jit(solution)/shard_map/pallas_call | solution.py:476
  72.3 3.0 %copy.10 = f32[8,32,16,128]{3,2,1,0:T(8,128)} copy(f32[8,32,16,128]{3,2,1,0:T(8,128)} %shard_map.64) | data formatting | bytes 4194304
where the time goes:
time: 75.5 us; the launch traced here: 75.4 us
  Pallas kernels  71 us (94%)
  local copies, waits for them, and re-layouts  3.05 us (4%)
  between operations  1.3 us (2%)
    pallas_call x1, Pallas kernels, on_device(): pl.pallas_call(functools.partial(kernel, nx, ny), out_shape=jax.ShapeDtyp...  71 us
    unnamed x1, local copies, waits for them, and re-layouts  3.05 us

commit v1 on v0

--- a/solution.py
+++ b/solution.py
@@ -13,8 +13,7 @@
 WEIGHT_SCALE = 1.0 / 65536.0
 TINY = 1e-30
 MESH = pl.DeviceIdType.MESH
-DIGITS = {32: ((4, 1), (2, 4), (4, 8)), 8: ((2, 1), (2, 2), (2, 4))}
-CUTS = (2, 12, 19, 28)
+CUT = 12
 
 
 def limited(upper, lower):
@@ -71,17 +70,17 @@
 
 
 def kernel(
-    nx, ny, shift_ref, weight_ref, rho_ref, vel_ref, mag_ref, pre_ref, out_ref,
-    u0, u1, w, wh, sd, sl, sf, pack, patch, xg, yg, st00, st01, st02, st10, st11, st12, ts, tb,
-    xs, xr, ys, yr, cs, cr, tsem, trec,
+    nx, ny, shift_ref, weight_ref, rho_in, vel_in, mag_in, pre_in, out_ref, rho_ref, vel_ref, mag_ref, pre_ref,
+    u0, u1, w, wh, sd, sl, sf, pack, patch, xg, yg, out0, ring0, back0, got0, out1, ring1, back1, got1,
+    xs, xr, ys, yr, ss, sr, ls,
 ):
     rows, nz, wide = rho_ref.shape
     half = nz // 2
     total_x = nx * rows
     total_y = ny * wide
     omega = 1.0 / (SHEAR_Q * total_x)
-    digits = DIGITS[ny]
-    stages = ((st00, st01, st02), (st10, st11, st12))
+    share = 32 // ny
+    spread = ((out0, ring0, back0, got0), (out1, ring1, back1, got1))
     gx = lax.axis_index("gx")
     gy = lax.axis_index("gy")
     first = gx == 0
@@ -90,16 +89,19 @@
     other = jnp.where(first, nx - 1, 0)
     north = lax.rem(gy + 1, ny)
     south = lax.rem(gy + ny - 1, ny)
-    mine = [lax.rem(lax.div(gy, stride), radix) for radix, stride in digits]
     lane = lax.broadcasted_iota(jnp.int32, (2, half, wide), 2)
     quad = jnp.bitwise_and(lane, 3)
-    group = lax.shift_right_logical(lane, 2)
+    even = jnp.bitwise_and(lane, 4) == 0
     inside = jnp.logical_and(lane >= 2, lane < wide - 2)
 
-    def digit_peer(stage, step):
-        radix, stride = digits[stage]
-        digit = lax.rem(mine[stage] + step, radix)
-        return digit, gy + (digit - mine[stage]) * stride
+    loads = [
+        pltpu.make_async_copy(src, dst, ls.at[k])
+        for k, (src, dst) in enumerate(
+            [(rho_in, rho_ref), (vel_in, vel_ref), (mag_in, mag_ref), (pre_in, pre_ref)]
+        )
+    ]
+    for load in loads:
+        load.start()
 
     barrier = pltpu.get_barrier_semaphore()
 
@@ -117,18 +119,23 @@
     def _():
         greet(gx + 1, gy)
 
-    far = 3 + sum(radix - 1 for radix, _ in digits)
+    def each(low, high, do):
+        def body(t, carry):
+            do(t)
+            return carry
+
+        lax.fori_loop(low, high, body, 0)
+
+    def peer(step):
+        return lax.rem(gy + step, ny)
 
     @pl.when(edge)
     def _():
-        for stage in range(3):
-            for step in range(1, digits[stage][0]):
-                greet(gx, digit_peer(stage, step)[1])
-        for y in (south, gy, north):
-            greet(other, y)
+        each(1, ny, lambda step: greet(gx, peer(step)))
+        each(0, ny, lambda step: greet(other, peer(step)))
 
     def await_greetings():
-        pl.semaphore_wait(barrier, jnp.where(edge, 3 + far, 4))
+        pl.semaphore_wait(barrier, jnp.where(edge, 2 + 2 * ny, 4))
 
     def remote(src, dst, send, recv, x, y):
         return pltpu.make_async_remote_copy(
@@ -143,21 +150,24 @@
             w[k, i + 2] = prim[k]
             wh[k, i + 2] = 0.5 * prim[k]
 
-    def collect(i, prim, packs):
-        turn = jnp.bitwise_and(4 * i + 4, wide - 1)
-        here = group == i
-        after = group == jnp.bitwise_and(i + 1, wide // 4 - 1)
-        moved = [pltpu.roll(prim[k], turn, 2) for k in range(8)]
-        left = [jnp.where(after, moved[k], packs[k]) for k in range(8)]
-        right = [jnp.where(here, moved[k], packs[8 + k]) for k in range(8)]
-        return (*left, *right)
-
-    def store_packs(sec, packs):
-        for k in range(8):
-            pack[sec, 0, k] = pltpu.roll(packs[k], wide - 4, 2)
-            pack[sec, 1, k] = packs[8 + k]
-
-    def start_row(i, packs):
+    def store_packs(sec):
+        def some(t, carry):
+            for k in (2 * t, 2 * t + 1):
+                both = []
+                for odd in range(2):
+                    acc = jnp.zeros((2, half, wide), jnp.float32)
+                    slot = lax.shift_right_logical(jnp.bitwise_and(lane - 4 * odd, wide - 1), 3)
+                    for i in range(odd, rows, 2):
+                        moved = pltpu.roll(w[k, i + 2], (4 * i + 4) % wide, 2)
+                        acc = jnp.where(slot == i // 2, moved, acc)
+                    both.append(acc)
+                pack[sec, 0, k] = pltpu.roll(jnp.where(even, both[1], both[0]), wide - 4, 2)
+                pack[sec, 1, k] = jnp.where(even, both[0], both[1])
+            return carry
+
+        lax.fori_loop(0, 4, some, 0)
+
+    def start_row(i):
         def load(ref, *lead):
             return jnp.stack([ref[(*lead, i, pl.ds(z, half, stride=2), slice(None))] for z in range(2)])
 
@@ -173,26 +183,23 @@
             u0[k, i] = value
         prim = [rho, *v, *b, p]
         put_primitive(i, prim)
-        return collect(i, prim, packs)
 
     def merged(i, ref, k):
         back = pltpu.roll(patch[k], jnp.bitwise_and(wide - 2 - 4 * i, wide - 1), 2)
         return ref[k, i] + jnp.where(inside, 0.0, back)
 
-    def middle_row(i, packs):
+    def middle_row(i):
         u = [merged(i, u1, k) for k in range(8)]
         for k in range(8):
             u1[k, i] = u[k]
         prim = to_primitive(u)
         put_primitive(i, prim)
-        return collect(i, prim, packs)
-
-    def final_row(i, carry):
+
+    def final_row(i):
         for k in range(8):
             value = merged(i, u0, k)
             for z in range(2):
                 out_ref[k, i, pl.ds(z, half, stride=2), :] = value[z]
-        return carry
 
     def z_up(x):
         return jnp.stack([x[1], pltpu.roll(x[0], half - 1, 0)])
@@ -302,87 +309,79 @@
     shift = shift_ref[0]
     weight = weight_ref[0].astype(jnp.float32) * WEIGHT_SCALE
     out_shift = jnp.where(first, total_y - 1 - shift, shift)
-    in_shift = jnp.where(first, shift, total_y - 1 - shift)
-    in_weight = jnp.where(first, weight, 1.0 - weight)
-    blocks = lax.div(out_shift, wide)
-    picks = []
-    for d, (radix, _) in enumerate(digits):
-        part = lax.rem(blocks, radix)
-        picks.append(lax.rem(mine[d] - part + radix, radix))
-        blocks = lax.div(blocks, radix) + (mine[d] < part).astype(jnp.int32)
-
-    def stage_copies(sec, stage, incoming):
-        ref = stages[sec][stage]
-        copies = []
-        for step in range(1, digits[stage][0]):
-            digit, y = digit_peer(stage, step)
-            slot = digit if incoming else mine[stage]
-            copies.append(
-                remote(
-                    ref.at[mine[stage]], ref.at[slot],
-                    cs.at[sec, stage, step - 1], cr.at[sec, stage, slot], gx, y,
-                )
-            )
-        return copies
-
-    def transit_copies(sec):
-        return [
-            remote(ts.at[sec], tb.at[sec, 0], tsem.at[sec, 0], trec.at[sec, 0], other, gy),
-            remote(ts.at[sec], tb.at[sec, 1], tsem.at[sec, 1], trec.at[sec, 1], other, north),
-        ]
+    out_weight = jnp.where(first, 1.0 - weight, weight)
+
+    def gather_copy(sec, step):
+        out, ring, _, _ = spread[sec]
+        to = peer(step)
+        return remote(out.at[to], ring.at[gy], ss.at[sec, 0], sr.at[sec, 0], gx, to)
+
+    def hand_copy(sec, step):
+        _, _, back, got = spread[sec]
+        to = peer(step)
+        return remote(back.at[to], got.at[gy], ss.at[sec, 1], sr.at[sec, 1], other, to)
+
+    def all_gathered(sec):
+        out, ring, _, _ = spread[sec]
+        few = pl.ds(0, ny - 1)
+        return remote(out.at[few], ring.at[few], ss.at[sec, 0], sr.at[sec, 0], gx, north)
+
+    def all_handed(sec):
+        _, _, back, got = spread[sec]
+        return remote(back, got, ss.at[sec, 1], sr.at[sec, 1], other, gy)
+
+    def parts(q):
+        return q // 4, q // 2 % 2, q % 2
 
     def chain_start(sec, u):
-        @pl.when(first)
-        def _():
-            for k in range(8):
-                stages[sec][0][mine[0], k] = u[k, 0:2]
-
-        @pl.when(last)
-        def _():
-            for k in range(8):
-                stages[sec][0][mine[0], k] = u[k, rows - 2 : rows]
+        out, ring, _, _ = spread[sec]
+
+        def fill(row):
+            for q in range(32):
+                k, j, z = parts(q)
+                out[q // share, q % share] = u[k, row + j, z]
+
+        pl.when(first)(lambda: fill(0))
+        pl.when(last)(lambda: fill(rows - 2))
 
         @pl.when(edge)
         def _():
-            for copy in stage_copies(sec, 0, False):
-                copy.start()
-
-    def chain_step(sec, stage):
+            ring[gy] = out[gy]
+            each(1, ny, lambda step: gather_copy(sec, step).start())
+
+    def chain_middle(sec):
         @pl.when(edge)
         def _():
-            for copy in stage_copies(sec, stage, True):
-                copy.wait_recv()
-            for k in range(8):
-                value = stages[sec][stage][picks[stage], k]
-                if stage < 2:
-                    stages[sec][stage + 1][mine[stage + 1], k] = value
-                else:
-                    ts[sec, k] = value
-            for copy in stage_copies(sec, stage + 1, False) if stage < 2 else transit_copies(sec):
-                copy.start()
+            _, ring, back, _ = spread[sec]
+            all_gathered(sec).wait_recv()
+            blocks = lax.div(out_shift, wide)
+            inner = lax.rem(out_shift, wide)
+            src = lax.broadcasted_iota(jnp.int32, (wide, wide), 0)
+            dst = lax.broadcasted_iota(jnp.int32, (wide, wide), 1)
+            gap = dst - src - inner
+            near = jnp.where(gap == 0, 1.0 - out_weight, 0.0) + jnp.where(gap == 1, out_weight, 0.0)
+            far = jnp.where(gap == -wide, 1.0 - out_weight, 0.0) + jnp.where(gap == 1 - wide, out_weight, 0.0)
+
+            def times(offset, m):
+                x = jnp.stack([ring[lax.rem(j + 2 * ny - offset - blocks, ny)] for j in range(ny)])
+                x = x.reshape(32 * half, wide)
+                return jnp.dot(x, m, precision=lax.Precision.HIGHEST, preferred_element_type=jnp.float32)
+
+            back[...] = (times(0, near) + times(1, far)).reshape(ny, share, half, wide)
+            each(0, ny, lambda step: hand_copy(sec, step).start())
 
     def chain_end(sec):
         @pl.when(edge)
         def _():
-            for copy in transit_copies(sec):
-                copy.wait_recv()
-            inner = lax.rem(in_shift, wide)
-            src = lax.broadcasted_iota(jnp.int32, (wide, wide), 0)
-            dst = lax.broadcasted_iota(jnp.int32, (wide, wide), 1)
-            gap = dst - src - inner
-            near = jnp.where(gap == 0, 1.0 - in_weight, 0.0) + jnp.where(gap == 1, in_weight, 0.0)
-            back = jnp.where(gap == -wide, 1.0 - in_weight, 0.0) + jnp.where(gap == 1 - wide, in_weight, 0.0)
-            flat = (8 * 2 * 2 * half, wide)
-
-            def times(x, m):
-                return jnp.dot(x, m, precision=lax.Precision.HIGHEST, preferred_element_type=jnp.float32)
-
-            ghost = times(tb[sec, 0].reshape(flat), near) + times(tb[sec, 1].reshape(flat), back)
-            ghost = ghost.reshape(8, 2, 2, half, wide)
+            got = spread[sec][3]
+            all_handed(sec).wait_recv()
             delta = jnp.where(first, 1.0, -1.0)
             start = jnp.where(first, 0, rows + 2)
             for j in range(2):
-                u = [ghost[k, j] for k in range(8)]
+                u = []
+                for k in range(8):
+                    at = [4 * k + 2 * j + z for z in range(2)]
+                    u.append(jnp.stack([got[q // share, q % share] for q in at]))
                 momentum = u[2] + u[0] * delta
                 u[7] = u[7] + u[2] * delta + 0.5 * u[0]
                 u[2] = momentum
@@ -402,31 +401,35 @@
     def on_side(side, do):
         pl.when(gx > 0 if side == 0 else gx < nx - 1)(do)
 
-    def outer_row(t):
-        return jnp.where(t < 2, t, t + rows - 4)
-
-    empty = tuple(jnp.zeros((2, half, wide), jnp.float32) for _ in range(16))
-
+    for load in loads:
+        load.wait()
     for sec in range(2):
         one_row = middle_row if sec else start_row
-        packs = lax.fori_loop(0, 4, lambda t, c: one_row(outer_row(t), c), empty)
+
+        def two_rows(t, carry):
+            one_row(2 * t)
+            one_row(2 * t + 1)
+            return carry
+
+        def outer_rows(t, carry):
+            return two_rows(t * (rows // 2 - 1), carry)
+
+        lax.fori_loop(0, 2, outer_rows, 0)
         if sec == 0:
             await_greetings()
         chain_start(sec, u1 if sec else u0)
         for side in range(2):
             on_side(side, lambda: x_copy(sec, side, False).start())
-        packs = lax.fori_loop(2, rows - 2, one_row, packs)
-        store_packs(sec, packs)
+        lax.fori_loop(1, rows // 2 - 1, two_rows, 0)
+        store_packs(sec)
         x_begin(2)
         for side in range(2):
             y_copy(sec, side, False).start()
         row = functools.partial(main_row, sec)
-        cuts = [min(c * rows // 32, rows - 2) for c in CUTS] + [rows - 2]
-        cuts[0] = 2
-        for stage in range(3):
-            lax.fori_loop(cuts[stage], cuts[stage + 1], row, 0)
-            chain_step(sec, stage)
-        lax.fori_loop(cuts[3], cuts[4], row, 0)
+        cut = min(CUT * rows // 32, rows - 2)
+        lax.fori_loop(2, cut, row, 0)
+        chain_middle(sec)
+        lax.fori_loop(cut, rows - 2, row, 0)
         for side in range(2):
             y_copy(sec, side, True).wait_recv()
         edge_patch(sec)
@@ -448,16 +451,13 @@
         for side in range(2):
             on_side(side, lambda: x_copy(sec, side, False).wait_send())
             y_copy(sec, side, False).wait_send()
-    lax.fori_loop(0, rows, final_row, 0)
+    each(0, rows // 2, lambda t: (final_row(2 * t), final_row(2 * t + 1)))
 
     @pl.when(edge)
     def _():
         for sec in range(2):
-            for stage in range(3):
-                for copy in stage_copies(sec, stage, False):
-                    copy.wait_send()
-            for copy in transit_copies(sec):
-                copy.wait_send()
+            all_gathered(sec).wait_send()
+            all_handed(sec).wait_send()
 
 
 def solution(mesh):
@@ -467,18 +467,22 @@
         rows, nz, wide = density.shape
         half = nz // 2
         tile = (2, half, wide)
-        radices = [radix for radix, _ in DIGITS[ny]]
         slab = (8, 2, *tile)
         f32 = jnp.float32
         dma = pltpu.SemaphoreType.DMA
         vmem = pl.BlockSpec(memory_space=pltpu.VMEM)
+        hbm = pl.BlockSpec(memory_space=pltpu.HBM)
         smem = pl.BlockSpec(memory_space=pltpu.SMEM)
         return pl.pallas_call(
             functools.partial(kernel, nx, ny),
             out_shape=jax.ShapeDtypeStruct((8, rows, nz, wide), f32),
-            in_specs=[smem, smem, vmem, vmem, vmem, vmem],
+            in_specs=[smem, smem, hbm, hbm, hbm, hbm],
             out_specs=vmem,
             scratch_shapes=[
+                pltpu.VMEM((rows, nz, wide), f32),
+                pltpu.VMEM((3, rows, nz, wide), f32),
+                pltpu.VMEM((3, rows, nz, wide), f32),
+                pltpu.VMEM((rows, nz, wide), f32),
                 pltpu.VMEM((8, rows, *tile), f32),
                 pltpu.VMEM((8, rows, *tile), f32),
                 pltpu.VMEM((8, rows + 4, *tile), f32),
@@ -490,20 +494,17 @@
                 pltpu.VMEM((8, *tile), f32),
                 pltpu.VMEM((2, 2, *slab), f32),
                 pltpu.VMEM((2, 2, 8, *tile), f32),
-                *[pltpu.VMEM((radix, *slab), f32) for radix in radices * 2],
-                pltpu.VMEM((2, *slab), f32),
-                pltpu.VMEM((2, 2, *slab), f32),
+                *[pltpu.VMEM((ny, 32 // ny, half, wide), f32) for _ in range(8)],
                 dma((2, 2)),
                 dma((2, 2)),
                 dma((2, 2)),
                 dma((2, 2)),
-                dma((2, 3, 3)),
-                dma((2, 3, 4)),
                 dma((2, 2)),
                 dma((2, 2)),
+                dma((4,)),
             ],
             compiler_params=pltpu.CompilerParams(
-                collective_id=0, has_side_effects=True, vmem_limit_bytes=60 * 1024 * 1024
+                collective_id=0, has_side_effects=True, vmem_limit_bytes=32 * 1024 * 1024
             ),
         )(shear_shift.reshape(1), remap_weight.reshape(1), density, velocity, bfield, pressure)
 

time: 75.5 us -> 50.9 us (0.67)
  the two profiles are of different devices: /device:TPU:8 before, /device:TPU:32 now
where the time goes in v1:
time: 50.9 us; the launch traced here: 50.6 us
  Pallas kernels  43.8 us (86%)
  local copies, waits for them, and re-layouts  5.48 us (11%)
  between operations  1.32 us (3%)
    pallas_call x1, Pallas kernels, on_device(): pl.pallas_call(functools.partial(kernel, nx, ny), out_shape=jax.ShapeDtyp...  43.8 us
    unnamed x9, local copies, waits for them, and re-layouts  5.48 us

profile of v1, /device:TPU:32, one launch (start us, length us, event | category | flops | bytes accessed | tf_op | source)
XLA Modules:
  0.0 50.6 jit_solution(18280698820458330941)
XLA Ops:
  1.3 0.0 copy-start
  1.3 1.1 %copy-done = f32[3,32,16,128]{3,2,1,0:T(8,128)S(1)} copy-done((f32[3,32,16,128]{3,2,1,0:T(8,128)S(1)}, f32[3,32,16,128]{3,2,1,0:T(8,128)}, u32[]{:S(2)}) %copy-start) | copy-done | bytes 786456
  2.4 0.0 copy-start.1
  2.4 1.1 %copy-done.1 = f32[3,32,16,128]{3,2,1,0:T(8,128)S(1)} copy-done((f32[3,32,16,128]{3,2,1,0:T(8,128)S(1)}, f32[3,32,16,128]{3,2,1,0:T(8,128)}, u32[]{:S(2)}) %copy-start.1) | copy-done | bytes 786456
  3.6 0.0 copy-start.2
  3.6 0.9 %copy-done.2 = f32[32,16,128]{2,1,0:T(8,128)S(1)} copy-done((f32[32,16,128]{2,1,0:T(8,128)S(1)}, f32[32,16,128]{2,1,0:T(8,128)}, u32[]{:S(2)}) %copy-start.2) | copy-done | bytes 262168
  4.5 0.0 copy-start.3
  4.5 0.9 %copy-done.3 = f32[32,16,128]{2,1,0:T(8,128)S(1)} copy-done((f32[32,16,128]{2,1,0:T(8,128)S(1)}, f32[32,16,128]{2,1,0:T(8,128)}, u32[]{:S(2)}) %copy-start.3) | copy-done | bytes 262168
  5.5 43.8 %shard_map.64 = f32[8,32,16,128]{3,2,1,0:T(8,128)S(1)} custom-call(s32[1]{0:T(128)} %bitcast.2.shift_ref, s32[1]{0:T(128)} %bitcast.3.weight_ref, f32[32,16,128]{2,1,0:T(8,128)S(1)} %copy-done.2, f32[3,32,16,128]{3,2,1,0:T(8,128)S(1)} %copy-done, f32[3,32,16,128]{3,2,1,0:T(8,128)S(1)} %copy-done.1, f32[32,16,128]{2,1,0:T(8,128)S(1)} %copy-done.3), custom_call_target="tpu_custom_call" | custom-call | tf_op jit(solution)/shard_map/pallas_call | solution.py:476
  49.3 1.3 %copy.10 = f32[8,32,16,128]{3,2,1,0:T(8,128)} copy(f32[8,32,16,128]{3,2,1,0:T(8,128)S(1)} %shard_map.64) | data formatting | bytes 4194304
Async XLA Ops:
  1.3 1.1 %copy-start = (f32[3,32,16,128]{3,2,1,0:T(8,128)S(1)}, f32[3,32,16,128]{3,2,1,0:T(8,128)}, u32[]{:S(2)}) copy-start(f32[3,32,16,128]{3,2,1,0:T(8,128)} %vel_in.1) | copy-start | bytes 2359300
  2.4 1.1 %copy-start.1 = (f32[3,32,16,128]{3,2,1,0:T(8,128)S(1)}, f32[3,32,16,128]{3,2,1,0:T(8,128)}, u32[]{:S(2)}) copy-start(f32[3,32,16,128]{3,2,1,0:T(8,128)} %mag_in.1) | copy-start | bytes 2359300
  3.6 0.9 %copy-start.2 = (f32[32,16,128]{2,1,0:T(8,128)S(1)}, f32[32,16,128]{2,1,0:T(8,128)}, u32[]{:S(2)}) copy-start(f32[32,16,128]{2,1,0:T(8,128)} %rho_in.1) | copy-start | bytes 786436
  4.5 0.9 %copy-start.3 = (f32[32,16,128]{2,1,0:T(8,128)S(1)}, f32[32,16,128]{2,1,0:T(8,128)}, u32[]{:S(2)}) copy-start(f32[32,16,128]{2,1,0:T(8,128)} %pre_in.1) | copy-start | bytes 786436

commit v2 on v1

--- a/solution.py
+++ b/solution.py
@@ -13,52 +13,52 @@
 WEIGHT_SCALE = 1.0 / 65536.0
 TINY = 1e-30
 MESH = pl.DeviceIdType.MESH
-CUT = 12
+CUTS = (12, 6, 18)
 
 
 def limited(upper, lower):
     return jnp.minimum(jnp.maximum(upper, jnp.minimum(lower, 0.0)), jnp.maximum(lower, 0.0))
 
 
-def side_flux(state, n):
+def side_terms(state, n):
     rho, v, b, p = state[0], state[1:4], state[4:7], state[7]
     a, c = [t for t in range(3) if t != n]
-    m = [rho * v[t] for t in range(3)]
-    vn, bn = v[n], b[n]
-    bn2 = bn * bn
+    bn2 = b[n] * b[n]
     bt2 = b[a] * b[a] + b[c] * b[c]
-    b2 = bt2 + bn2
-    hb2 = 0.5 * b2
-    pg = p + 0.5 * (p + (m[0] * v[0] + m[1] * v[1] + m[2] * v[2]))
-    energy = pg + hb2
-    fba = vn * b[a] - bn * v[a]
-    fbc = vn * b[c] - bn * v[c]
+    hb2 = 0.5 * (bt2 + bn2)
+    pt = p + hb2
+    energy = pt + 0.5 * (p + rho * (v[0] * v[0] + v[1] * v[1] + v[2] * v[2]))
+    hgp = (0.5 * GAMMA) * p
+    spread = hgp - hb2
+    inner = spread * spread + (GAMMA * p) * bt2
+    square = (hgp + hb2) + inner * lax.rsqrt(jnp.maximum(inner, TINY))
+    fast = square * lax.rsqrt(jnp.maximum(rho * square, TINY))
+    return pt - bn2, energy, jnp.abs(v[n]) + fast
+
+
+def side_flux(state, n, terms, speed):
+    rho, v, b = state[0], state[1:4], state[4:7]
+    a, c = [t for t in range(3) if t != n]
+    stress, energy, _ = terms
+    drift = v[n] + speed
+    mass = rho * drift
+    wa, wc = b[n] * v[a], b[n] * v[c]
     flux = [None] * 8
-    flux[0] = m[n]
-    flux[1 + n] = m[n] * vn - bn2 + (p + hb2)
-    flux[1 + a] = m[n] * v[a] - bn * b[a]
-    flux[1 + c] = m[n] * v[c] - bn * b[c]
-    flux[4 + a] = fba
-    flux[4 + c] = fbc
-    flux[7] = (pg + p) * vn + (b[a] * fba + b[c] * fbc)
-    gp = GAMMA * p
-    total = gp + b2
-    spread = gp - b2
-    inner = spread * spread + (4.0 * GAMMA * p) * bt2
-    twice = total + inner * lax.rsqrt(jnp.maximum(inner, TINY))
-    fast = twice * lax.rsqrt(jnp.maximum((rho + rho) * twice, TINY))
-    return flux, [rho, *m, *b, energy], jnp.abs(vn) + fast
+    flux[0] = mass
+    flux[1 + n] = mass * v[n] + stress
+    flux[1 + a] = mass * v[a] - b[n] * b[a]
+    flux[1 + c] = mass * v[c] - b[n] * b[c]
+    flux[4 + a] = drift * b[a] - wa
+    flux[4 + c] = drift * b[c] - wc
+    flux[7] = (energy * drift + stress * v[n]) - (b[a] * wa + b[c] * wc)
+    return flux
 
 
 def face_flux(left, right, n):
-    fl, ul, sl = side_flux(left, n)
-    fr, ur, sr = side_flux(right, n)
-    speed = jnp.maximum(sl, sr)
-    out = []
-    for k in range(8):
-        jump = speed * (ur[k] - ul[k])
-        out.append(-jump if fl[k] is None else (fl[k] + fr[k]) - jump)
-    return out
+    tl, tr = side_terms(left, n), side_terms(right, n)
+    speed = jnp.maximum(tl[2], tr[2])
+    fl, fr = side_flux(left, n, tl, speed), side_flux(right, n, tr, -speed)
+    return [speed * (left[k] - right[k]) if k == 4 + n else fl[k] + fr[k] for k in range(8)]
 
 
 def to_primitive(u):
@@ -71,7 +71,7 @@
 
 def kernel(
     nx, ny, shift_ref, weight_ref, rho_in, vel_in, mag_in, pre_in, out_ref, rho_ref, vel_ref, mag_ref, pre_ref,
-    u0, u1, w, wh, sd, sl, sf, pack, patch, xg, yg, out0, ring0, back0, got0, out1, ring1, back1, got1,
+    u0, u1, w0, wh0, w1, wh1, sd0, sl0, sf0, sd1, sl1, sf1, pack, patch, xg, yg, out0, ring0, back0, got0, out1, ring1, back1, got1,
     xs, xr, ys, yr, ss, sr, ls,
 ):
     rows, nz, wide = rho_ref.shape
@@ -80,6 +80,8 @@
     total_y = ny * wide
     omega = 1.0 / (SHEAR_Q * total_x)
     share = 32 // ny
+    prims, halves = (w0, w1), (wh0, wh1)
+    carried = ((sd0, sl0, sf0), (sd1, sl1, sf1))
     spread = ((out0, ring0, back0, got0), (out1, ring1, back1, got1))
     gx = lax.axis_index("gx")
     gy = lax.axis_index("gy")
@@ -145,10 +147,10 @@
     def radial(i):
         return (gx * rows + i).astype(jnp.float32) + (0.5 - 0.5 * total_x)
 
-    def put_primitive(i, prim):
-        for k in range(8):
-            w[k, i + 2] = prim[k]
-            wh[k, i + 2] = 0.5 * prim[k]
+    def put_primitive(sec, i, prim):
+        for k in range(8):
+            prims[sec][k, i + 2] = prim[k]
+            halves[sec][k, i + 2] = 0.5 * prim[k]
 
     def store_packs(sec):
         def some(t, carry):
@@ -158,7 +160,7 @@
                     acc = jnp.zeros((2, half, wide), jnp.float32)
                     slot = lax.shift_right_logical(jnp.bitwise_and(lane - 4 * odd, wide - 1), 3)
                     for i in range(odd, rows, 2):
-                        moved = pltpu.roll(w[k, i + 2], (4 * i + 4) % wide, 2)
+                        moved = pltpu.roll(prims[sec][k, i + 2], (4 * i + 4) % wide, 2)
                         acc = jnp.where(slot == i // 2, moved, acc)
                     both.append(acc)
                 pack[sec, 0, k] = pltpu.roll(jnp.where(even, both[1], both[0]), wide - 4, 2)
@@ -181,8 +183,7 @@
         energy = p * (1.0 / (GAMMA - 1.0)) + 0.5 * (kin + mag)
         for k, value in enumerate([rho, *m, *b, energy]):
             u0[k, i] = value
-        prim = [rho, *v, *b, p]
-        put_primitive(i, prim)
+        put_primitive(0, i, [rho, *v, *b, p])
 
     def merged(i, ref, k):
         back = pltpu.roll(patch[k], jnp.bitwise_and(wide - 2 - 4 * i, wide - 1), 2)
@@ -192,8 +193,7 @@
         u = [merged(i, u1, k) for k in range(8)]
         for k in range(8):
             u1[k, i] = u[k]
-        prim = to_primitive(u)
-        put_primitive(i, prim)
+        put_primitive(1, i, to_primitive(u))
 
     def final_row(i):
         for k in range(8):
@@ -223,7 +223,9 @@
         face = face_flux(left, right, n)
         return [f - down(f) for f in face]
 
-    def x_face(i):
+    def x_face(sec, i):
+        w, wh = prims[sec], halves[sec]
+        sd, sl, _ = carried[sec]
         left, right = [], []
         for k in range(8):
             d = wh[k, i + 4] - wh[k, i + 3]
@@ -235,22 +237,25 @@
             sl[k] = here + h
         return face_flux(left, right, 0)
 
-    def x_begin(i):
+    def x_begin(sec, i):
+        w, wh = prims[sec], halves[sec]
+        sd, sl, sf = carried[sec]
         for k in range(8):
             before = wh[k, i + 1] - wh[k, i]
             d = wh[k, i + 2] - wh[k, i + 1]
             sd[k] = d
             sl[k] = w[k, i + 1] + limited(d, before)
-        face = x_face(i - 1)
+        face = x_face(sec, i - 1)
         for k in range(8):
             sf[k] = face[k]
 
     def main_row(sec, i, carry):
-        whole = [w[k, i + 2] for k in range(8)]
-        halved = [wh[k, i + 2] for k in range(8)]
+        sf = carried[sec][2]
+        whole = [prims[sec][k, i + 2] for k in range(8)]
+        halved = [halves[sec][k, i + 2] for k in range(8)]
         dz = periodic(whole, halved, 2, z_up, z_down)
         dy = periodic(whole, halved, 1, y_up, y_down)
-        fx = x_face(i)
+        fx = x_face(sec, i)
         change = []
         for k in range(8):
             change.append((dz[k] + jnp.where(inside, dy[k], 0.0)) + (fx[k] - sf[k]))
@@ -385,10 +390,11 @@
                 momentum = u[2] + u[0] * delta
                 u[7] = u[7] + u[2] * delta + 0.5 * u[0]
                 u[2] = momentum
-                put_primitive(start + j - 2, to_primitive(u))
+                put_primitive(sec, start + j - 2, to_primitive(u))
 
     def x_copy(sec, side, incoming):
         away = gx - 1 if side == 0 else gx + 1
+        w = prims[sec]
         own = w.at[:, 2:4] if side == 0 else w.at[:, rows : rows + 2]
         slot = side if incoming else 1 - side
         return remote(own, xg.at[sec, slot], xs.at[sec, side], xr.at[sec, slot], away, gy)
@@ -401,56 +407,86 @@
     def on_side(side, do):
         pl.when(gx > 0 if side == 0 else gx < nx - 1)(do)
 
-    for load in loads:
-        load.wait()
-    for sec in range(2):
+    def two_rows(sec):
         one_row = middle_row if sec else start_row
 
-        def two_rows(t, carry):
+        def body(t):
             one_row(2 * t)
             one_row(2 * t + 1)
-            return carry
-
-        def outer_rows(t, carry):
-            return two_rows(t * (rows // 2 - 1), carry)
-
-        lax.fori_loop(0, 2, outer_rows, 0)
+
+        return body
+
+    def outer_rows(sec):
+        each(0, 2, lambda t: two_rows(sec)(t * (rows // 2 - 1)))
         if sec == 0:
             await_greetings()
         chain_start(sec, u1 if sec else u0)
         for side in range(2):
             on_side(side, lambda: x_copy(sec, side, False).start())
-        lax.fori_loop(1, rows // 2 - 1, two_rows, 0)
+
+    def send_columns(sec):
         store_packs(sec)
-        x_begin(2)
         for side in range(2):
             y_copy(sec, side, False).start()
-        row = functools.partial(main_row, sec)
-        cut = min(CUT * rows // 32, rows - 2)
-        lax.fori_loop(2, cut, row, 0)
-        chain_middle(sec)
-        lax.fori_loop(cut, rows - 2, row, 0)
+
+    def take_columns(sec):
         for side in range(2):
             y_copy(sec, side, True).wait_recv()
         edge_patch(sec)
+
+    def take_rows(sec):
         for side in range(2):
 
             def take():
                 x_copy(sec, side, True).wait_recv()
+                start = 0 if side == 0 else rows + 2
                 for k in range(8):
                     value = xg[sec, side, k]
-                    start = 0 if side == 0 else rows + 2
-                    w[k, start : start + 2] = value
-                    wh[k, start : start + 2] = 0.5 * value
+                    prims[sec][k, start : start + 2] = value
+                    halves[sec][k, start : start + 2] = 0.5 * value
 
             on_side(side, take)
         chain_end(sec)
-        lax.fori_loop(rows - 2, rows, row, 0)
-        x_begin(0)
-        lax.fori_loop(0, 2, row, 0)
+
+    def sent(sec):
         for side in range(2):
             on_side(side, lambda: x_copy(sec, side, False).wait_send())
             y_copy(sec, side, False).wait_send()
+
+    def main(sec, low, high):
+        lax.fori_loop(low, high, functools.partial(main_row, sec), 0)
+
+    cuts = [min(c * rows // 32, rows - 4) for c in CUTS]
+    cuts = [cuts[0], max(cuts[1], 4), max(cuts[2], 4)]
+    for load in loads:
+        load.wait()
+    outer_rows(0)
+    each(1, rows // 2 - 1, two_rows(0))
+    send_columns(0)
+    x_begin(0, 2)
+    main(0, 2, cuts[0])
+    chain_middle(0)
+    main(0, cuts[0], rows - 2)
+    take_columns(0)
+    each(1, rows // 2 - 1, two_rows(1))
+    x_begin(1, 4)
+    main(1, 4, cuts[1])
+    take_rows(0)
+    main(0, rows - 2, rows)
+    x_begin(0, 0)
+    main(0, 0, 2)
+    outer_rows(1)
+    send_columns(1)
+    main(1, cuts[1], cuts[2])
+    chain_middle(1)
+    main(1, cuts[2], rows - 2)
+    take_columns(1)
+    take_rows(1)
+    main(1, rows - 2, rows)
+    x_begin(1, 0)
+    main(1, 0, 4)
+    sent(0)
+    sent(1)
     each(0, rows // 2, lambda t: (final_row(2 * t), final_row(2 * t + 1)))
 
     @pl.when(edge)
@@ -485,11 +521,8 @@
                 pltpu.VMEM((rows, nz, wide), f32),
                 pltpu.VMEM((8, rows, *tile), f32),
                 pltpu.VMEM((8, rows, *tile), f32),
-                pltpu.VMEM((8, rows + 4, *tile), f32),
-                pltpu.VMEM((8, rows + 4, *tile), f32),
-                pltpu.VMEM((8, *tile), f32),
-                pltpu.VMEM((8, *tile), f32),
-                pltpu.VMEM((8, *tile), f32),
+                *[pltpu.VMEM((8, rows + 4, *tile), f32) for _ in range(4)],
+                *[pltpu.VMEM((8, *tile), f32) for _ in range(6)],
                 pltpu.VMEM((2, 2, 8, *tile), f32),
                 pltpu.VMEM((8, *tile), f32),
                 pltpu.VMEM((2, 2, *slab), f32),
@@ -506,7 +539,14 @@
             compiler_params=pltpu.CompilerParams(
                 collective_id=0, has_side_effects=True, vmem_limit_bytes=32 * 1024 * 1024
             ),
-        )(shear_shift.reshape(1), remap_weight.reshape(1), density, velocity, bfield, pressure)
+        )(
+            shear_shift.reshape(1),
+            remap_weight.reshape(1),
+            *[
+                pltpu.with_memory_space_constraint(x, pltpu.HBM)
+                for x in (density, velocity, bfield, pressure)
+            ],
+        )
 
     placed = (
         P("gx", None, "gy"),

time: 50.9 us -> 46.3 us (0.910)
  local copies, waits for them, and re-layouts: 5.48 us -> 1.32 us
    unnamed x9 -> x1, local copies, waits for them, and re-layouts: 5.48 us -> 1.32 us
where the time goes in v2:
time: 46.3 us; the launch traced here: 46.2 us
  Pallas kernels  43.6 us (94%)
  local copies, waits for them, and re-layouts  1.32 us (3%)
  between operations  1.3 us (3%)
    pallas_call x1, Pallas kernels, on_device(): pl.pallas_call(functools.partial(kernel, nx, ny), out_shape=jax.ShapeDtyp...  43.6 us
    unnamed x1, local copies, waits for them, and re-layouts  1.32 us

profile of v2, /device:TPU:32, one launch (start us, length us, event | category | flops | bytes accessed | tf_op | source)
XLA Modules:
  0.0 46.2 jit_solution(16376822020147269534)
XLA Ops:
  1.3 43.6 %shard_map.64 = f32[8,32,16,128]{3,2,1,0:T(8,128)S(1)} custom-call(s32[1]{0:T(128)} %bitcast.2.shift_ref, s32[1]{0:T(128)} %bitcast.3.weight_ref, f32[32,16,128]{2,1,0:T(8,128)} %rho_in.1, f32[3,32,16,128]{3,2,1,0:T(8,128)} %vel_in.1, f32[3,32,16,128]{3,2,1,0:T(8,128)} %mag_in.1, f32[32,16,128]{2,1,0:T(8,128)} %pre_in.1), custom_call_target="tpu_custom_call" | custom-call | tf_op jit(solution)/shard_map/pallas_call | solution.py:512
  44.9 1.3 %copy.10 = f32[8,32,16,128]{3,2,1,0:T(8,128)} copy(f32[8,32,16,128]{3,2,1,0:T(8,128)S(1)} %shard_map.64) | data formatting | bytes 4194304

commit v3 on v2

--- a/solution.py
+++ b/solution.py
@@ -13,7 +13,7 @@
 WEIGHT_SCALE = 1.0 / 65536.0
 TINY = 1e-30
 MESH = pl.DeviceIdType.MESH
-CUTS = (12, 6, 18)
+CUTS = (4, 14, 6, 16)
 
 
 def limited(upper, lower):
@@ -71,7 +71,7 @@
 
 def kernel(
     nx, ny, shift_ref, weight_ref, rho_in, vel_in, mag_in, pre_in, out_ref, rho_ref, vel_ref, mag_ref, pre_ref,
-    u0, u1, w0, wh0, w1, wh1, sd0, sl0, sf0, sd1, sl1, sf1, pack, patch, xg, yg, out0, ring0, back0, got0, out1, ring1, back1, got1,
+    u0, u1, w0, wh0, w1, wh1, ylo, yhi, sd0, sl0, sf0, sd1, sl1, sf1, pack, patch, xg, yg, out0, ring0, back0, got0, out1, ring1, back1, got1,
     xs, xr, ys, yr, ss, sr, ls,
 ):
     rows, nz, wide = rho_ref.shape
@@ -121,6 +121,10 @@
     def _():
         greet(gx + 1, gy)
 
+    def to_all(low, do):
+        for step in range(low, ny):
+            do(step)
+
     def each(low, high, do):
         def body(t, carry):
             do(t)
@@ -129,15 +133,15 @@
         lax.fori_loop(low, high, body, 0)
 
     def peer(step):
-        return lax.rem(gy + step, ny)
+        return jnp.bitwise_and(gy + step, ny - 1)
 
     @pl.when(edge)
     def _():
-        each(1, ny, lambda step: greet(gx, peer(step)))
-        each(0, ny, lambda step: greet(other, peer(step)))
+        to_all(1, lambda step: greet(gx, peer(step)))
+        greet(other, gy)
 
     def await_greetings():
-        pl.semaphore_wait(barrier, jnp.where(edge, 2 + 2 * ny, 4))
+        pl.semaphore_wait(barrier, jnp.where(edge, 3 + ny, 4))
 
     def remote(src, dst, send, recv, x, y):
         return pltpu.make_async_remote_copy(
@@ -154,7 +158,7 @@
 
     def store_packs(sec):
         def some(t, carry):
-            for k in (2 * t, 2 * t + 1):
+            for k in [4 * t + j for j in range(4)]:
                 both = []
                 for odd in range(2):
                     acc = jnp.zeros((2, half, wide), jnp.float32)
@@ -167,7 +171,15 @@
                 pack[sec, 1, k] = jnp.where(even, both[0], both[1])
             return carry
 
-        lax.fori_loop(0, 4, some, 0)
+        lax.fori_loop(0, 2, some, 0)
+
+    def y_states(i, prim):
+        for k in range(8):
+            half_prim = 0.5 * prim[k]
+            d = y_up(half_prim) - half_prim
+            h = limited(d, y_down(d))
+            ylo[k, i] = prim[k] + h
+            yhi[k, i] = y_up(prim[k] - h)
 
     def start_row(i):
         def load(ref, *lead):
@@ -183,7 +195,9 @@
         energy = p * (1.0 / (GAMMA - 1.0)) + 0.5 * (kin + mag)
         for k, value in enumerate([rho, *m, *b, energy]):
             u0[k, i] = value
-        put_primitive(0, i, [rho, *v, *b, p])
+        prim = [rho, *v, *b, p]
+        put_primitive(0, i, prim)
+        y_states(i, prim)
 
     def merged(i, ref, k):
         back = pltpu.roll(patch[k], jnp.bitwise_and(wide - 2 - 4 * i, wide - 1), 2)
@@ -193,7 +207,9 @@
         u = [merged(i, u1, k) for k in range(8)]
         for k in range(8):
             u1[k, i] = u[k]
-        put_primitive(1, i, to_primitive(u))
+        prim = to_primitive(u)
+        put_primitive(1, i, prim)
+        y_states(i, prim)
 
     def final_row(i):
         for k in range(8):
@@ -213,15 +229,15 @@
     def y_down(x):
         return pltpu.roll(x, 1, 2)
 
-    def periodic(whole, halved, n, up, down):
+    def z_change(whole, halved):
         left, right = [], []
         for k in range(8):
-            d = up(halved[k]) - halved[k]
-            h = limited(d, down(d))
+            d = z_up(halved[k]) - halved[k]
+            h = limited(d, z_down(d))
             left.append(whole[k] + h)
-            right.append(up(whole[k] - h))
-        face = face_flux(left, right, n)
-        return [f - down(f) for f in face]
+            right.append(z_up(whole[k] - h))
+        face = face_flux(left, right, 2)
+        return [f - z_down(f) for f in face]
 
     def x_face(sec, i):
         w, wh = prims[sec], halves[sec]
@@ -253,8 +269,9 @@
         sf = carried[sec][2]
         whole = [prims[sec][k, i + 2] for k in range(8)]
         halved = [halves[sec][k, i + 2] for k in range(8)]
-        dz = periodic(whole, halved, 2, z_up, z_down)
-        dy = periodic(whole, halved, 1, y_up, y_down)
+        dz = z_change(whole, halved)
+        fy = face_flux([ylo[k, i] for k in range(8)], [yhi[k, i] for k in range(8)], 1)
+        dy = [f - y_down(f) for f in fy]
         fx = x_face(sec, i)
         change = []
         for k in range(8):
@@ -352,7 +369,11 @@
         @pl.when(edge)
         def _():
             ring[gy] = out[gy]
-            each(1, ny, lambda step: gather_copy(sec, step).start())
+
+    def chain_send(sec):
+        @pl.when(edge)
+        def _():
+            to_all(1, lambda step: gather_copy(sec, step).start())
 
     def chain_middle(sec):
         @pl.when(edge)
@@ -373,7 +394,7 @@
                 return jnp.dot(x, m, precision=lax.Precision.HIGHEST, preferred_element_type=jnp.float32)
 
             back[...] = (times(0, near) + times(1, far)).reshape(ny, share, half, wide)
-            each(0, ny, lambda step: hand_copy(sec, step).start())
+            to_all(0, lambda step: hand_copy(sec, step).start())
 
     def chain_end(sec):
         @pl.when(edge)
@@ -407,25 +428,22 @@
     def on_side(side, do):
         pl.when(gx > 0 if side == 0 else gx < nx - 1)(do)
 
-    def two_rows(sec):
-        one_row = middle_row if sec else start_row
-
-        def body(t):
-            one_row(2 * t)
-            one_row(2 * t + 1)
-
-        return body
+    def some_rows(sec, listed):
+        for i in listed:
+            (middle_row if sec else start_row)(i)
 
     def outer_rows(sec):
-        each(0, 2, lambda t: two_rows(sec)(t * (rows // 2 - 1)))
-        if sec == 0:
-            await_greetings()
-        chain_start(sec, u1 if sec else u0)
+        some_rows(sec, (0, 1, rows - 2, rows - 1))
+
+    def inner_rows(sec):
+        each(0, rows // 4 - 1, lambda t: some_rows(sec, [4 * t + 2 + j for j in range(4)]))
+
+    def send_rows(sec):
+        chain_send(sec)
         for side in range(2):
             on_side(side, lambda: x_copy(sec, side, False).start())
 
     def send_columns(sec):
-        store_packs(sec)
         for side in range(2):
             y_copy(sec, side, False).start()
 
@@ -456,38 +474,56 @@
     def main(sec, low, high):
         lax.fori_loop(low, high, functools.partial(main_row, sec), 0)
 
-    cuts = [min(c * rows // 32, rows - 4) for c in CUTS]
-    cuts = [cuts[0], max(cuts[1], 4), max(cuts[2], 4)]
+    cuts = [min(max(c * rows // 32, 4), rows - 4) for c in CUTS]
     for load in loads:
         load.wait()
     outer_rows(0)
-    each(1, rows // 2 - 1, two_rows(0))
-    send_columns(0)
+    inner_rows(0)
+    chain_start(0, u0)
+    store_packs(0)
     x_begin(0, 2)
     main(0, 2, cuts[0])
+    await_greetings()
+    send_rows(0)
+    send_columns(0)
+    main(0, cuts[0], cuts[1])
     chain_middle(0)
-    main(0, cuts[0], rows - 2)
+    main(0, cuts[1], rows - 2)
     take_columns(0)
-    each(1, rows // 2 - 1, two_rows(1))
+    inner_rows(1)
     x_begin(1, 4)
-    main(1, 4, cuts[1])
+    main(1, 4, cuts[2])
     take_rows(0)
     main(0, rows - 2, rows)
     x_begin(0, 0)
     main(0, 0, 2)
     outer_rows(1)
+    chain_start(1, u1)
+    send_rows(1)
+    store_packs(1)
     send_columns(1)
-    main(1, cuts[1], cuts[2])
+    main(1, cuts[2], cuts[3])
     chain_middle(1)
-    main(1, cuts[2], rows - 2)
+    main(1, cuts[3], rows - 2)
     take_columns(1)
+    state = [[ref[k] for k in range(8)] for ref in carried[1]]
+    for saved, ref in zip(state, carried[0]):
+        for k in range(8):
+            ref[k] = saved[k]
+    x_begin(1, 2)
+    main(1, 2, 4)
+    each(1, rows // 2 - 1, lambda t: (final_row(2 * t), final_row(2 * t + 1)))
     take_rows(1)
+    for saved, ref in zip(carried[0], carried[1]):
+        for k in range(8):
+            ref[k] = saved[k]
     main(1, rows - 2, rows)
     x_begin(1, 0)
-    main(1, 0, 4)
+    main(1, 0, 2)
+    for i in (0, 1, rows - 2, rows - 1):
+        final_row(i)
     sent(0)
     sent(1)
-    each(0, rows // 2, lambda t: (final_row(2 * t), final_row(2 * t + 1)))
 
     @pl.when(edge)
     def _():
@@ -522,6 +558,7 @@
                 pltpu.VMEM((8, rows, *tile), f32),
                 pltpu.VMEM((8, rows, *tile), f32),
                 *[pltpu.VMEM((8, rows + 4, *tile), f32) for _ in range(4)],
+                *[pltpu.VMEM((8, rows, *tile), f32) for _ in range(2)],
                 *[pltpu.VMEM((8, *tile), f32) for _ in range(6)],
                 pltpu.VMEM((2, 2, 8, *tile), f32),
                 pltpu.VMEM((8, *tile), f32),
@@ -537,7 +574,7 @@
                 dma((4,)),
             ],
             compiler_params=pltpu.CompilerParams(
-                collective_id=0, has_side_effects=True, vmem_limit_bytes=32 * 1024 * 1024
+                collective_id=0, has_side_effects=True, vmem_limit_bytes=40 * 1024 * 1024
             ),
         )(
             shear_shift.reshape(1),

time: 46.3 us -> 42.3 us (0.914)
  Pallas kernels: 43.6 us -> 39.6 us
    pallas_call x1, Pallas kernels: 43.6 us -> 39.6 us  [on_device(): pl.pallas_call(functools.partial(kernel, nx, ny), out_shape=jax.ShapeDtyp...]
where the time goes in v3:
time: 42.3 us; the launch traced here: 42.2 us
  Pallas kernels  39.6 us (94%)
  local copies, waits for them, and re-layouts  1.32 us (3%)
  between operations  1.3 us (3%)
    pallas_call x1, Pallas kernels, on_device(): pl.pallas_call(functools.partial(kernel, nx, ny), out_shape=jax.ShapeDtyp...  39.6 us
    unnamed x1, local copies, waits for them, and re-layouts  1.32 us

profile of v3, /device:TPU:32, one launch (start us, length us, event | category | flops | bytes accessed | tf_op | source)
XLA Modules:
  0.0 42.2 jit_solution(3437165257885781038)
XLA Ops:
  1.3 39.6 %shard_map.64 = f32[8,32,16,128]{3,2,1,0:T(8,128)S(1)} custom-call(s32[1]{0:T(128)} %bitcast.2.shift_ref, s32[1]{0:T(128)} %bitcast.3.weight_ref, f32[32,16,128]{2,1,0:T(8,128)} %rho_in.1, f32[3,32,16,128]{3,2,1,0:T(8,128)} %vel_in.1, f32[3,32,16,128]{3,2,1,0:T(8,128)} %mag_in.1, f32[32,16,128]{2,1,0:T(8,128)} %pre_in.1), custom_call_target="tpu_custom_call" | custom-call | tf_op jit(solution)/shard_map/pallas_call | solution.py:548
  40.9 1.3 %copy.10 = f32[8,32,16,128]{3,2,1,0:T(8,128)} copy(f32[8,32,16,128]{3,2,1,0:T(8,128)S(1)} %shard_map.64) | data formatting | bytes 4194304

commit v4 on v3

--- a/solution.py
+++ b/solution.py
@@ -13,7 +13,7 @@
 WEIGHT_SCALE = 1.0 / 65536.0
 TINY = 1e-30
 MESH = pl.DeviceIdType.MESH
-CUTS = (4, 14, 6, 16)
+CUTS = (14, 6, 16)
 
 
 def limited(upper, lower):
@@ -439,7 +439,6 @@
         each(0, rows // 4 - 1, lambda t: some_rows(sec, [4 * t + 2 + j for j in range(4)]))
 
     def send_rows(sec):
-        chain_send(sec)
         for side in range(2):
             on_side(side, lambda: x_copy(sec, side, False).start())
 
@@ -451,6 +450,9 @@
         for side in range(2):
             y_copy(sec, side, True).wait_recv()
         edge_patch(sec)
+
+    early = jnp.where(last, 0, rows - 2)
+    late = jnp.where(last, rows - 2, 0)
 
     def take_rows(sec):
         for side in range(2):
@@ -464,7 +466,12 @@
                     halves[sec][k, start : start + 2] = 0.5 * value
 
             on_side(side, take)
-        chain_end(sec)
+
+    def boundary_rows(sec, start):
+        x_begin(sec, start)
+        main(sec, start, start + 2)
+        for j in range(2):
+            (final_row if sec else middle_row)(start + j)
 
     def sent(sec):
         for side in range(2):
@@ -478,50 +485,43 @@
     for load in loads:
         load.wait()
     outer_rows(0)
+    chain_start(0, u0)
     inner_rows(0)
-    chain_start(0, u0)
+    await_greetings()
+    chain_send(0)
     store_packs(0)
     x_begin(0, 2)
-    main(0, 2, cuts[0])
-    await_greetings()
+    main(0, 2, 8 * rows // 32)
     send_rows(0)
     send_columns(0)
-    main(0, cuts[0], cuts[1])
+    main(0, 8 * rows // 32, cuts[0])
     chain_middle(0)
-    main(0, cuts[1], rows - 2)
+    main(0, cuts[0], rows - 2)
     take_columns(0)
     inner_rows(1)
     x_begin(1, 4)
-    main(1, 4, cuts[2])
+    main(1, 4, cuts[1])
     take_rows(0)
-    main(0, rows - 2, rows)
-    x_begin(0, 0)
-    main(0, 0, 2)
-    outer_rows(1)
+    boundary_rows(0, early)
+    chain_end(0)
+    boundary_rows(0, late)
     chain_start(1, u1)
+    chain_send(1)
+    store_packs(1)
+    main(1, cuts[1], cuts[2] - 4 * rows // 32)
     send_rows(1)
-    store_packs(1)
     send_columns(1)
-    main(1, cuts[2], cuts[3])
+    main(1, cuts[2] - 4 * rows // 32, cuts[2])
     chain_middle(1)
-    main(1, cuts[3], rows - 2)
+    main(1, cuts[2], rows - 2)
     take_columns(1)
-    state = [[ref[k] for k in range(8)] for ref in carried[1]]
-    for saved, ref in zip(state, carried[0]):
-        for k in range(8):
-            ref[k] = saved[k]
     x_begin(1, 2)
     main(1, 2, 4)
     each(1, rows // 2 - 1, lambda t: (final_row(2 * t), final_row(2 * t + 1)))
     take_rows(1)
-    for saved, ref in zip(carried[0], carried[1]):
-        for k in range(8):
-            ref[k] = saved[k]
-    main(1, rows - 2, rows)
-    x_begin(1, 0)
-    main(1, 0, 2)
-    for i in (0, 1, rows - 2, rows - 1):
-        final_row(i)
+    boundary_rows(1, early)
+    chain_end(1)
+    boundary_rows(1, late)
     sent(0)
     sent(1)
 

time: 42.3 us -> 40.4 us (0.955)
  Pallas kernels: 39.6 us -> 37.7 us
    pallas_call x1, Pallas kernels: 39.6 us -> 37.7 us  [on_device(): pl.pallas_call(functools.partial(kernel, nx, ny), out_shape=jax.ShapeDtyp...]
where the time goes in v4:
time: 40.4 us; the launch traced here: 40.3 us
  Pallas kernels  37.7 us (93%)
  local copies, waits for them, and re-layouts  1.32 us (3%)
  between operations  1.3 us (3%)
    pallas_call x1, Pallas kernels, on_device(): pl.pallas_call(functools.partial(kernel, nx, ny), out_shape=jax.ShapeDtyp...  37.7 us
    unnamed x1, local copies, waits for them, and re-layouts  1.32 us

profile of v4, /device:TPU:32, one launch (start us, length us, event | category | flops | bytes accessed | tf_op | source)
XLA Modules:
  0.0 40.3 jit_solution(4075177110033576866)
XLA Ops:
  1.3 37.7 %shard_map.64 = f32[8,32,16,128]{3,2,1,0:T(8,128)S(1)} custom-call(s32[1]{0:T(128)} %bitcast.2.shift_ref, s32[1]{0:T(128)} %bitcast.3.weight_ref, f32[32,16,128]{2,1,0:T(8,128)} %rho_in.1, f32[3,32,16,128]{3,2,1,0:T(8,128)} %vel_in.1, f32[3,32,16,128]{3,2,1,0:T(8,128)} %mag_in.1, f32[32,16,128]{2,1,0:T(8,128)} %pre_in.1), custom_call_target="tpu_custom_call" | custom-call | tf_op jit(solution)/shard_map/pallas_call | solution.py:548
  39.0 1.3 %copy.10 = f32[8,32,16,128]{3,2,1,0:T(8,128)} copy(f32[8,32,16,128]{3,2,1,0:T(8,128)S(1)} %shard_map.64) | data formatting | bytes 4194304
